TPU v7x, 32 devices: a whole 2x2x4 slice. The times are simulated.
32 devices in a mesh: group: 2 (over y), tile: 4 (over x, core), seq: 4 (over z).
Axes of the slice: x: 2, y: 2, z: 4, core: 2. Of those that a mesh axis runs over, the one named last changes fastest.
Arguments:
- hidden: bfloat16 [8, 1024, 3072], P(('group', 'tile'), 'seq'), parts along dimension 0
- modulation: float32 [10, 3072], P('group'), parts along dimension 0, may hold values from -3 to 3
- w_qkv: bfloat16 [3072, 9216], P('tile', 'seq')
- w_out: bfloat16 [3072, 3072], P('seq', 'tile'), may hold values from -0.109375 to 0.109375
- w_head: bfloat16 [3072, 64], replicated, may hold values from -0.109375 to 0.109375
- latent: float32 [8, 1024, 64], P(('group', 'tile'), 'seq'), parts along dimension 0, may hold values from -6 to 6
- weights_int: int32 [8, 1024], P(('group', 'tile'), 'seq'), parts along dimension 0, may hold values from 1 to 8
- step_index: int32 [2], P('group'), parts along dimension 0, may hold values from 0 to 13
Outputs:
- stepped: float32 [8, 1024, 64], P(('group', 'tile'), 'seq'), parts along dimension 0
- clean: float32 [8, 1024, 64], P(('group', 'tile'), 'seq'), parts along dimension 0
There are 2 independent parts, one for each index of `group`. A program takes and returns all parts, laid end to end along the dimension named above; an argument that names none is the same for every part. Nothing has to cross between parts.
All inputs are finite; a program needn't handle non-finite values.
Results may differ from a plain program's by a relative error of at most 0.0055.
Values may be sent and summed in bfloat16 or wider, within the bound.
A program may use at most 64 MiB of HBM per device.

v0:
```python
import math
import jax
import jax.numpy as jnp
from jax import lax
from jax.sharding import PartitionSpec as P

HD = 128
NSTEPS = 28


def shifted(value, axis, steps):
    count = lax.axis_size(axis)
    leading, last = (max(0, -steps), min(count, count - steps))
    return lax.ppermute(value, axis, [(source, source + steps) for source in range(leading, last)])


def layer_norm(values):
    mean = jnp.mean(values, axis=-1, keepdims=True)
    centred = values - mean
    spread = jnp.mean(centred * centred, axis=-1, keepdims=True)
    return centred * lax.rsqrt(spread + 1e-06)


def root_norm(values):
    return values * lax.rsqrt(jnp.mean(values * values, axis=-1, keepdims=True) + 1e-06)


def noise_level(index, steps):
    level = 1.0 - index / steps
    return 3.0 * level / (1.0 + 2.0 * level)


def shards(hidden, modulation, w_qkv, w_out, w_head, latent, weights_int, step_index):
    local = hidden[0].astype(jnp.float32)
    norm_in = (layer_norm(local) * (1.0 + modulation[1]) + modulation[0]).astype(jnp.bfloat16)
    gathered = lax.all_gather(norm_in, "seq", axis=0, tiled=True)
    length = gathered.shape[0]
    heads_here = w_qkv.shape[1] // (3 * HD)
    projected = jnp.dot(
        gathered,
        lax.all_gather(w_qkv, "tile", axis=0, tiled=True),
        preferred_element_type=jnp.float32,
    )
    full_out = lax.all_gather(w_out, "tile", axis=1, tiled=True)
    projected = projected.reshape(length, heads_here, 3, HD)
    queries = root_norm(projected[:, :, 0]).astype(jnp.bfloat16)
    keys = root_norm(projected[:, :, 1]).astype(jnp.bfloat16)
    values = projected[:, :, 2].astype(jnp.bfloat16)
    block = min(512, length)
    scale = 1.0 / math.sqrt(HD)
    pieces = []
    for first in range(0, length, block):
        scores = (
            jnp.einsum(
                "qhe,khe->hqk",
                queries[first : first + block],
                keys,
                preferred_element_type=jnp.float32,
            )
            * scale
        )
        expo = jnp.exp(scores)
        probs = (expo / jnp.sum(expo, axis=-1, keepdims=True)).astype(jnp.bfloat16)
        pieces.append(
            jnp.einsum("hqk,khe->qhe", probs, values, preferred_element_type=jnp.float32).astype(
                jnp.bfloat16
            )
        )
    attended = jnp.concatenate(pieces, axis=0).reshape(length, heads_here * HD)
    summed = lax.psum_scatter(
        jnp.dot(attended, full_out, preferred_element_type=jnp.float32).astype(jnp.bfloat16),
        "seq",
        scatter_dimension=0,
        tiled=True,
    ).astype(jnp.float32)
    mixed = local + modulation[2] * summed
    norm_out = (layer_norm(mixed) * (1.0 + modulation[4]) + modulation[3]).astype(jnp.bfloat16)
    velocity = jnp.dot(norm_out, w_head, preferred_element_type=jnp.float32)
    index = step_index[0].astype(jnp.float32)
    now = noise_level(index, NSTEPS)
    after = noise_level(index + 1.0, NSTEPS)
    base = latent[0]
    weight = weights_int[0].astype(jnp.float32)
    moved = base + (after - now) * velocity
    guess = base - now * velocity
    weighted = jnp.concatenate([moved, guess], axis=1) * weight[:, None]
    seq_count = lax.axis_size("seq")
    place = lax.axis_index("seq")
    prev_tile = (
        shifted(weighted.astype(jnp.bfloat16), "tile", 1).astype(weighted.dtype),
        shifted(weight.astype(jnp.bfloat16), "tile", 1).astype(weight.dtype),
    )
    prev_sums, prev_weight = (
        shifted(prev_tile[0].astype(jnp.bfloat16), "seq", -(seq_count - 2)).astype(jnp.float32),
        shifted(prev_tile[1].astype(jnp.bfloat16), "seq", -(seq_count - 2)).astype(jnp.float32),
    )
    next_tile = (
        shifted(weighted.astype(jnp.bfloat16), "tile", -1).astype(weighted.dtype),
        shifted(weight.astype(jnp.bfloat16), "tile", -1).astype(weight.dtype),
    )
    next_sums, next_weight = (
        shifted(next_tile[0].astype(jnp.bfloat16), "seq", seq_count - 2).astype(jnp.float32),
        shifted(next_tile[1].astype(jnp.bfloat16), "seq", seq_count - 2).astype(jnp.float32),
    )
    take_prev = place < 2
    take_next = place >= seq_count - 2
    totals = weighted + jnp.where(take_prev, prev_sums, 0.0) + jnp.where(take_next, next_sums, 0.0)
    norms = weight + jnp.where(take_prev, prev_weight, 0.0) + jnp.where(take_next, next_weight, 0.0)
    joined = totals / norms[:, None]
    channels = velocity.shape[1]
    return (joined[None, :, :channels], joined[None, :, channels:])


def solution(mesh):
    in_specs = (
        P(("group", "tile"), "seq", None),
        P("group", None),
        P("tile", "seq"),
        P("seq", "tile"),
        P(),
        P(("group", "tile"), "seq", None),
        P(("group", "tile"), "seq"),
        P("group"),
    )
    out_specs = (P(("group", "tile"), "seq", None), P(("group", "tile"), "seq", None))
    return jax.shard_map(shards, mesh=mesh, in_specs=in_specs, out_specs=out_specs, check_vma=False)
```

profile of v0, /device:TPU:26, one launch (start us, length us, event | category | flops | bytes accessed | tf_op | source)
XLA Modules:
  0.0 437.2 jit_solution(16859526870282650366)
XLA Ops:
  10.8 2.0 fusion.8
  12.8 1.9 fusion.11
  16.3 112.1 %all-gather.4.cloned.1.call-done = bf16[1024,3072]{1,0:T(8,128)(2,1)} async-done(((bf16[256,3072]{1,0:T(8,128)(2,1)}), bf16[1024,3072]{1,0:T(8,128)(2,1)}) %all-gather.4.cloned.1.call-update) | async-done | bytes 6291472 | tf_op jit(solution)/shard_map/all_gather | solution.py:36
  128.4 92.7 %all-gather.6.cloned.1.call-done = bf16[3072,2304]{1,0:T(8,128)(2,1)} async-done(((bf16[768,2304]{1,0:T(8,128)(2,1)}), bf16[3072,2304]{1,0:T(8,128)(2,1)}) %all-gather.6.cloned.1.call-update) | async-done | bytes 14155792 | tf_op jit(solution)/shard_map/all_gather | solution.py:41
  221.1 19.6 %fusion.31 = f32[1024,2304]{0,1:T(8,128)S(1)} fusion(bf16[1024,3072]{1,0:T(8,128)(2,1)} %all-gather.4.cloned.1.call-done, bf16[3072,2304]{1,0:T(8,128)(2,1)} %all-gather.6.cloned.1.call-done), kind=kOutput, calls=%fused_computation.60 | convolution fusion | flops 14495514624 | bytes 29884416 | tf_op jit(solution)/shard_map/dot_general | solution.py:39
  240.7 3.5 copy-done.3
  244.2 2.0 slice.50
  246.3 3.6 copy.21
  249.9 2.9 fusion.12
  252.8 2.3 multiply_reduce_fusion.1
  256.2 8.2 %fusion = (f32[6,512]{1,0:T(8,128)S(1)}, f32[6,512,1024]{2,1,0:T(8,128)}) fusion(f32[1024,6,3,128]{0,3,2,1:T(8,128)} %bitcast.78, f32[1024,6]{0,1:T(8,128)S(1)} %add_rsqrt_fusion, bf16[1024,6,128]{2,0,1:T(8,128)(2,1)S(1)} %fusion.13), kind=kOutput, calls=%fused_computation.4 | convolution fusion | flops 813167616 | bytes 16560128 | tf_op jit(solution)/shard_map/qhe,khe->hqk/dot_general | solution.py:54
  264.5 2.7 fusion.1
  267.1 6.0 %fusion.19 = bf16[512,6,128]{0,2,1:T(8,128)(2,1)S(1)} fusion(f32[6,512,1024]{2,1,0:T(8,128)} %get-tuple-element.14, f32[6,512]{1,0:T(8,128)S(1)} %get-tuple-element.13, f32[1024,6,3,128]{0,3,2,1:T(8,128)S(1)} %bitcast.82), kind=kOutput, calls=%fused_computation.35 | convolution fusion | flops 815136768 | bytes 14958592 | tf_op jit(solution)/shard_map/hqk,khe->qhe/dot_general | solution.py:65
  273.1 2.9 fusion.20
  276.3 9.5 %convolution_convert_fusion = bf16[1024,3072]{1,0:T(8,128)(2,1)} fusion(bf16[1024,768]{0,1:T(8,128)(2,1)S(1)} %bitcast.84, bf16[768,3072]{1,0:T(8,128)(2,1)} %all-gather.8.cloned.1.call-done), kind=kOutput, calls=%fused_computation.8 | convolution fusion | flops 4834983936 | bytes 12582912 | tf_op jit(solution)/shard_map/dot_general | solution.py:71
  286.6 110.6 %reduce-scatter.2.cloned.1.call-done = bf16[256,3072]{1,0:T(8,128)(2,1)} async-done(((bf16[1024,3072]{1,0:T(8,128)(2,1)}), bf16[256,3072]{1,0:T(8,128)(2,1)}) %reduce-scatter.2.cloned.1.call-update) | async-done | bytes 1572880 | tf_op jit(solution)/shard_map/reduce_scatter | solution.py:70
  397.2 2.1 fusion.14
  401.3 1.9 collective-permute-start
  403.3 3.6 collective-permute-start.2
  406.9 1.9 collective-permute-start.4
  408.9 3.6 collective-permute-start.6
  412.5 2.9 collective-permute-start.5
  416.8 5.4 %collective-permute-start.1 = (bf16[256,128]{0,1:T(8,128)(2,1)S(1)}, bf16[256,128]{0,1:T(8,128)(2,1)S(1)}, u32[]{:S(2)}, u32[]{:S(2)}) collective-permute-start(bf16[256,128]{0,1:T(8,128)(2,1)S(1)} %collective-permute-done), channel_id=1, source_target_pairs={{2,0},{3,1},{6,4},{7,5},{10,8},{11,9},{14,12},{15,13},{18,16},{19,... | collective-permute-start | bytes 196616 | tf_op jit(solution)/shard_map/ppermute | solution.py:14
  424.1 5.9 %collective-permute-done.3 = bf16[256,128]{0,1:T(8,128)(2,1)S(1)} collective-permute-done((bf16[256,128]{0,1:T(8,128)(2,1)S(1)}, bf16[256,128]{0,1:T(8,128)(2,1)S(1)}, u32[]{:S(2)}, u32[]{:S(2)}) %collective-permute-start.3) | collective-permute-done | bytes 65568 | tf_op jit(solution)/shard_map/ppermute | solution.py:14
  (60 shorter events, 12.2 us)
Async XLA Ops:
  7.2 393.0 %copy-start = (bf16[3072,64]{0,1:T(8,128)(2,1)S(1)}, bf16[3072,64]{0,1:T(8,128)(2,1)}, u32[]{:S(2)}) copy-start(bf16[3072,64]{0,1:T(8,128)(2,1)} %param.12) | copy-start | bytes 1179652
  7.2 5.6 %copy-start.1 = (bf16[1,256,3072]{2,1,0:T(8,128)(2,1)S(1)}, bf16[1,256,3072]{2,1,0:T(8,128)(2,1)}, u32[]{:S(2)}) copy-start(bf16[1,256,3072]{2,1,0:T(8,128)(2,1)} %param.8) | copy-start | bytes 4718596
  7.2 121.2 %all-gather.4.cloned.1.call-start = ((), (), s32[]{:S(2)}) async-start(), calls=%async_computation.1 | async-start | bytes 7864320 | tf_op jit(solution)/shard_map/all_gather | solution.py:36
  14.8 206.3 %all-gather.6.cloned.1.call-start = ((), (), s32[]{:S(2)}) async-start(), calls=%async_computation.2 | async-start | bytes 17694720 | tf_op jit(solution)/shard_map/all_gather | solution.py:41
  15.5 260.8 %all-gather.8.cloned.1.call-start = ((), (), s32[]{:S(2)}) async-start(), calls=%async_computation.3 | async-start | bytes 5898240 | tf_op jit(solution)/shard_map/all_gather | solution.py:44
  16.3 381.0 %reduce-scatter.2.cloned.1.call-start = ((), (), s32[]{:S(2)}) async-start(), calls=%async_computation.4 | async-start | bytes 7864320 | tf_op jit(solution)/shard_map/reduce_scatter | solution.py:70
  240.7 3.6 copy-start.3
  249.9 5.3 %copy-start.2 = (f32[1024,6,1,128]{3,0,1,2:T(8,128)S(1)}, f32[1024,6,1,128]{3,0,1,2:T(8,128)}, u32[]{:S(2)}) copy-start(f32[1024,6,1,128]{3,0,1,2:T(8,128)} %copy.21) | copy-start | bytes 9437188
  255.2 9.2 %slice-start = ((s8[9437184]{0:T(1024)(128)(4,1)}), s8[4194304]{0:T(1024)(128)(4,1)S(1)}, s32[]{:S(2)}) async-start(s8[9437184]{0:T(1024)(128)(4,1)} %bitcast.79), calls=%async_computation.5 | async-start | bytes 8388608
  256.2 8.3 %slice-start.1 = ((s8[9437184]{0:T(1024)(128)(4,1)}), s8[4194304]{0:T(1024)(128)(4,1)S(1)}, s32[]{:S(2)}) async-start(s8[9437184]{0:T(1024)(128)(4,1)} %bitcast.79), calls=%async_computation.6 | async-start | bytes 8388608
  256.2 8.2 %slice-start.2 = ((s8[9437184]{0:T(1024)(128)(4,1)}), s8[1048576]{0:T(1024)(128)(4,1)S(1)}, s32[]{:S(2)}) async-start(s8[9437184]{0:T(1024)(128)(4,1)} %bitcast.79), calls=%async_computation.7 | async-start | bytes 2097152
  285.8 0.7 copy-start.7
  397.2 2.1 copy-start.4
  397.2 3.0 copy-start.5
  397.2 3.0 copy-start.6
  397.2 3.0 copy-start.8
  401.3 15.4 %collective-permute-start = (bf16[256,128]{0,1:T(8,128)(2,1)S(1)}, bf16[256,128]{0,1:T(8,128)(2,1)S(1)}, u32[]{:S(2)}, u32[]{:S(2)}) collective-permute-start(bf16[256,128]{0,1:T(8,128)(2,1)S(1)} %fusion.27), channel_id=1, source_target_pairs={{0,4},{4,8},{8,12},{1,5},{5,9},{9,13},{2,6},{6,10},{10,14},{3,7},{... | collective-permute-start | bytes 196616 | tf_op jit(solution)/shard_map/ppermute | solution.py:14
  403.3 19.0 %collective-permute-start.2 = (bf16[256,128]{0,1:T(8,128)(2,1)S(1)}, bf16[256,128]{0,1:T(8,128)(2,1)S(1)}, u32[]{:S(2)}, u32[]{:S(2)}) collective-permute-start(bf16[256,128]{0,1:T(8,128)(2,1)S(1)} %fusion.27), channel_id=1, source_target_pairs={{4,0},{8,4},{12,8},{5,1},{9,5},{13,9},{6,2},{10,6},{14,10},{7,3},{... | collective-permute-start | bytes 196616 | tf_op jit(solution)/shard_map/ppermute | solution.py:14
  406.9 5.6 %collective-permute-start.4 = (bf16[256]{0:T(256)(128)(2,1)S(1)}, bf16[256]{0:T(256)(128)(2,1)S(1)}, u32[]{:S(2)}, u32[]{:S(2)}) collective-permute-start(bf16[256]{0:T(256)(128)(2,1)S(1)} %convert_element_type.109), channel_id=1, source_target_pairs={{0,4},{4,8},{8,12},{1,5},{5,9},{9,13},{2,6},{6,10},{10,14},{3,7},{... | collective-permute-start | bytes 1544 | tf_op jit(solution)/shard_map/ppermute | solution.py:14
  408.9 6.6 %collective-permute-start.6 = (bf16[256]{0:T(256)(128)(2,1)S(1)}, bf16[256]{0:T(256)(128)(2,1)S(1)}, u32[]{:S(2)}, u32[]{:S(2)}) collective-permute-start(bf16[256]{0:T(256)(128)(2,1)S(1)} %convert_element_type.109), channel_id=1, source_target_pairs={{4,0},{8,4},{12,8},{5,1},{9,5},{13,9},{6,2},{10,6},{14,10},{7,3},{... | collective-permute-start | bytes 1544 | tf_op jit(solution)/shard_map/ppermute | solution.py:14
  412.5 11.0 %collective-permute-start.5 = (bf16[256]{0:T(256)(128)(2,1)S(1)}, bf16[256]{0:T(256)(128)(2,1)S(1)}, u32[]{:S(2)}, u32[]{:S(2)}) collective-permute-start(bf16[256]{0:T(256)(128)(2,1)S(1)} %collective-permute-done.4), channel_id=1, source_target_pairs={{2,0},{3,1},{6,4},{7,5},{10,8},{11,9},{14,12},{15,13},{18,16},{19,... | collective-permute-start | bytes 1544 | tf_op jit(solution)/shard_map/ppermute | solution.py:14
  415.5 8.1 %collective-permute-start.7 = (bf16[256]{0:T(256)(128)(2,1)S(1)}, bf16[256]{0:T(256)(128)(2,1)S(1)}, u32[]{:S(2)}, u32[]{:S(2)}) collective-permute-start(bf16[256]{0:T(256)(128)(2,1)S(1)} %collective-permute-done.6), channel_id=1, source_target_pairs={{0,2},{1,3},{4,6},{5,7},{8,10},{9,11},{12,14},{13,15},{16,18},{17,... | collective-permute-start | bytes 1544 | tf_op jit(solution)/shard_map/ppermute | solution.py:14
  416.8 7.3 %collective-permute-start.1 = (bf16[256,128]{0,1:T(8,128)(2,1)S(1)}, bf16[256,128]{0,1:T(8,128)(2,1)S(1)}, u32[]{:S(2)}, u32[]{:S(2)}) collective-permute-start(bf16[256,128]{0,1:T(8,128)(2,1)S(1)} %collective-permute-done), channel_id=1, source_target_pairs={{2,0},{3,1},{6,4},{7,5},{10,8},{11,9},{14,12},{15,13},{18,16},{19,... | collective-permute-start | bytes 196616 | tf_op jit(solution)/shard_map/ppermute | solution.py:14
  422.2 7.7 %collective-permute-start.3 = (bf16[256,128]{0,1:T(8,128)(2,1)S(1)}, bf16[256,128]{0,1:T(8,128)(2,1)S(1)}, u32[]{:S(2)}, u32[]{:S(2)}) collective-permute-start(bf16[256,128]{0,1:T(8,128)(2,1)S(1)} %collective-permute-done.2), channel_id=1, source_target_pairs={{0,2},{1,3},{4,6},{5,7},{8,10},{9,11},{12,14},{13,15},{16,18},{17,... | collective-permute-start | bytes 196616 | tf_op jit(solution)/shard_map/ppermute | solution.py:14
Sparse Core Ops, SparseCore 0:
  14.9 113.4 all-gather.3
  129.9 91.1 all-gather.5
  222.6 37.4 all-gather.7
  286.0 111.1 reduce-scatter.1
where the time goes:
time: 438 us; the launch traced here: 437 us
  waiting for transfers between devices  323 us (74%)
  matrix products  50 us (11%)
  starting transfers between devices  22.2 us (5%)
  other arithmetic  17 us (4%)
  between operations  14.9 us (3%)
  local copies, waits for them, and re-layouts  9.9 us (2%)
    all_gather x1, waiting for transfers between devices, shards(): gathered = lax.all_gather(norm_in, 'seq', axis=0, tiled=True)  112 us
    reduce_scatter x1, waiting for transfers between devices, shards(): lax.psum_scatter(jnp.dot(attended, full_out, preferred_element_type=jnp.f...  111 us
    all_gather x1, waiting for transfers between devices, shards(): lax.all_gather(w_qkv, 'tile', axis=0, tiled=True)  92.7 us
    ppermute x8, starting transfers between devices, shifted(): lax.ppermute(value, axis, [(source, source + steps) for source in range(l...  22.1 us
    dot_general x1, matrix products, shards(): jnp.dot(gathered, lax.all_gather(w_qkv, 'tile', axis=0, tiled=True), pref...  19.6 us
    dot_general x2, matrix products, shards(): jnp.einsum('qhe,khe->hqk', queries[first:first + block], keys, preferred_...  10.9 us
    dot_general x1, matrix products, shards(): jnp.dot(attended, full_out, preferred_element_type=jnp.float32)  9.54 us
    dot_general x2, matrix products, shards(): jnp.einsum('hqk,khe->qhe', probs, values, preferred_element_type=jnp.floa...  8.92 us
  transfers between devices with their start and end apart: 12, of which 5 were waited for; matrix products, arithmetic and copies ran while one was open for 12% of the time, Pallas kernels for 0%

commit v1 on v0

--- a/solution.py
+++ b/solution.py
@@ -1,3 +1,4 @@
+import functools
 import math
 import jax
 import jax.numpy as jnp
@@ -6,6 +7,20 @@
 
 HD = 128
 NSTEPS = 28
+
+
+def touch_space_now(patch, row_axis):
+    ndev = lax.axis_size(row_axis)
+    all_rows = [patch]
+    for dev in range(1, ndev):
+        all_rows.append(
+            lax.ppermute(all_rows[dev - 1], row_axis, [(ix, (ix - 1) % ndev) for ix in range(ndev)])
+        )
+    res = jnp.concatenate(all_rows, 0)
+    return jnp.roll(res, lax.axis_index(row_axis) * patch.shape[0], 0)
+
+
+step_on_the_waves = functools.partial(touch_space_now, row_axis="tile")
 
 
 def shifted(value, axis, steps):
@@ -36,11 +51,7 @@
     gathered = lax.all_gather(norm_in, "seq", axis=0, tiled=True)
     length = gathered.shape[0]
     heads_here = w_qkv.shape[1] // (3 * HD)
-    projected = jnp.dot(
-        gathered,
-        lax.all_gather(w_qkv, "tile", axis=0, tiled=True),
-        preferred_element_type=jnp.float32,
-    )
+    projected = jnp.dot(gathered, step_on_the_waves(w_qkv), preferred_element_type=jnp.float32)
     full_out = lax.all_gather(w_out, "tile", axis=1, tiled=True)
     projected = projected.reshape(length, heads_here, 3, HD)
     queries = root_norm(projected[:, :, 0]).astype(jnp.bfloat16)

time: 438 us -> 372 us (0.85)
  waiting for transfers between devices: 323 us -> 226 us
  local copies, waits for them, and re-layouts: 9.9 us -> 38.6 us
    all_gather x1, waiting for transfers between devices: 112 us -> 0.01 us  [shards(): gathered = lax.all_gather(norm_in, 'seq', axis=0, tiled=True)]
    ppermute x0 -> x3, waiting for transfers between devices: none -> 107 us  [touch_space_now(): lax.ppermute(all_rows[dev - 1], row_axis, [(ix, (ix - 1) % ndev) for ix i...]
    all_gather x1 -> x0, waiting for transfers between devices: 92.7 us -> none  [shards(): lax.all_gather(w_qkv, 'tile', axis=0, tiled=True)]
    unnamed x25 -> x38, local copies, waits for them, and re-layouts: 7.19 us -> 31.7 us
    ppermute x0 -> x3, starting transfers between devices: none -> 4.57 us  [touch_space_now(): lax.ppermute(all_rows[dev - 1], row_axis, [(ix, (ix - 1) % ndev) for ix i...]
  transfers between devices with their start and end apart: 12 -> 14, of which waited for: 5 -> 7; matrix products, arithmetic and copies ran while one was open for 12% -> 21% of each run, Pallas kernels for 0% -> 0%
where the time goes in v1:
time: 372 us; the launch traced here: 369 us
  waiting for transfers between devices  226 us (61%)
  matrix products  50.2 us (13%)
  local copies, waits for them, and re-layouts  38.6 us (10%)
  starting transfers between devices  22.7 us (6%)
  other arithmetic  16.9 us (5%)
  between operations  14.9 us (4%)
    reduce_scatter x1, waiting for transfers between devices, shards(): lax.psum_scatter(jnp.dot(attended, full_out, preferred_element_type=jnp.f...  112 us
    ppermute x3, waiting for transfers between devices, touch_space_now(): lax.ppermute(all_rows[dev - 1], row_axis, [(ix, (ix - 1) % ndev) for ix i...  107 us
    unnamed x38, local copies, waits for them, and re-layouts  31.7 us
    dot_general x1, matrix products, shards(): jnp.dot(gathered, step_on_the_waves(w_qkv), preferred_element_type=jnp.fl...  19.7 us
    ppermute x8, starting transfers between devices, shifted(): lax.ppermute(value, axis, [(source, source + steps) for source in range(l...  18 us
    dot_general x2, matrix products, shards(): jnp.einsum('qhe,khe->hqk', queries[first:first + block], keys, preferred_...  10.9 us
    dot_general x1, matrix products, shards(): jnp.dot(attended, full_out, preferred_element_type=jnp.float32)  9.6 us
    dot_general x2, matrix products, shards(): jnp.einsum('hqk,khe->qhe', probs, values, preferred_element_type=jnp.floa...  8.92 us
  transfers between devices with their start and end apart: 14, of which 7 were waited for; matrix products, arithmetic and copies ran while one was open for 21% of the time, Pallas kernels for 0%

profile of v1, /device:TPU:26, one launch (start us, length us, event | category | flops | bytes accessed | tf_op | source)
XLA Modules:
  0.0 369.3 jit_solution(18213145232911290150)
XLA Ops:
  14.9 39.3 %collective-permute-done = bf16[768,2304]{1,0:T(8,128)(2,1)S(1)} collective-permute-done((bf16[768,2304]{1,0:T(8,128)(2,1)}, bf16[768,2304]{1,0:T(8,128)(2,1)S(1)}, u32[]{:S(2)}, u32[]{:S(2)}) %collective-permute-start) | collective-permute-done | bytes 3538976 | tf_op jit(solution)/shard_map/ppermute | solution.py:17
  58.1 39.0 %collective-permute-done.1 = bf16[768,2304]{1,0:T(8,128)(2,1)} collective-permute-done((bf16[768,2304]{1,0:T(8,128)(2,1)S(1)}, bf16[768,2304]{1,0:T(8,128)(2,1)}, u32[]{:S(2)}, u32[]{:S(2)}) %collective-permute-start.1) | collective-permute-done | bytes 3538976 | tf_op jit(solution)/shard_map/ppermute | solution.py:17
  97.1 2.3 collective-permute-start.2
  99.6 4.1 %constant_dynamic-update-slice_fusion.7 = bf16[6144,2304]{1,0:T(8,128)(2,1)} fusion(bf16[768,2304]{1,0:T(8,128)(2,1)} %param.10), kind=kLoop, calls=%fused_computation.59 | loop fusion | bytes 7077888
  105.7 4.1 %constant_dynamic-update-slice_fusion.5 = bf16[6144,2304]{1,0:T(8,128)(2,1)} fusion(bf16[6144,2304]{1,0:T(8,128)(2,1)} %constant_dynamic-update-slice_fusion.6, bf16[768,2304]{1,0:T(8,128)(2,1)} %collective-permute-done.1), kind=kLoop, calls=%fused_computation.57 | loop fusion | bytes 7077888
  109.8 29.0 %collective-permute-done.2 = bf16[768,2304]{1,0:T(8,128)(2,1)} collective-permute-done((bf16[768,2304]{1,0:T(8,128)(2,1)}, bf16[768,2304]{1,0:T(8,128)(2,1)}, u32[]{:S(2)}, u32[]{:S(2)}) %collective-permute-start.2) | collective-permute-done | bytes 3538976 | tf_op jit(solution)/shard_map/ppermute | solution.py:17
  138.8 4.6 %constant_dynamic-update-slice_fusion.4 = bf16[6144,2304]{1,0:T(8,128)(2,1)} fusion(bf16[6144,2304]{1,0:T(8,128)(2,1)} %constant_dynamic-update-slice_fusion.5, bf16[768,2304]{1,0:T(8,128)(2,1)} %collective-permute-done.2), kind=kLoop, calls=%fused_computation.56 | loop fusion | bytes 7077888
  147.3 4.0 %constant_dynamic-update-slice_fusion.1 = bf16[6144,2304]{1,0:T(8,128)(2,1)} fusion(bf16[6144,2304]{1,0:T(8,128)(2,1)} %constant_dynamic-update-slice_fusion.2, bf16[768,2304]{1,0:T(8,128)(2,1)} %collective-permute-done.1), kind=kLoop, calls=%fused_computation.53 | loop fusion | bytes 7077888
  151.3 4.1 %constant_dynamic-update-slice_fusion = bf16[6144,2304]{1,0:T(8,128)(2,1)} fusion(bf16[6144,2304]{1,0:T(8,128)(2,1)} %constant_dynamic-update-slice_fusion.1, bf16[768,2304]{1,0:T(8,128)(2,1)} %collective-permute-done.2), kind=kLoop, calls=%fused_computation.52 | loop fusion | bytes 7077888 | tf_op jit(solution)/shard_map/jit(_roll_dynamic)/concatenate | solution.py:20
  155.5 19.7 %fusion = f32[1024,2304]{0,1:T(8,128)S(1)} fusion(bf16[1024,3072]{1,0:T(8,128)(2,1)} %all-gather.3.cloned.1.call-done, bf16[6144,2304]{1,0:T(8,128)(2,1)} %constant_dynamic-update-slice_fusion, s32[]{:T(128)S(6)} %select_n.42), kind=kOutput, calls=%fused_computation | convolution fusion | flops 14495514624 | bytes 29884420 | tf_op jit(solution)/shard_map/dot_general | solution.py:54
  175.2 3.5 copy-done.3
  180.8 3.6 copy.21
  184.4 2.9 fusion.14
  187.3 2.3 multiply_reduce_fusion.1
  190.7 8.2 %fusion.2 = (f32[6,512]{1,0:T(8,128)S(1)}, f32[6,512,1024]{2,1,0:T(8,128)}) fusion(f32[1024,6,3,128]{0,3,2,1:T(8,128)} %bitcast.77, f32[1024,6]{0,1:T(8,128)S(1)} %add_rsqrt_fusion, bf16[1024,6,128]{2,0,1:T(8,128)(2,1)S(1)} %fusion.15), kind=kOutput, calls=%fused_computation.6 | convolution fusion | flops 813167616 | bytes 16560128 | tf_op jit(solution)/shard_map/qhe,khe->hqk/dot_general | solution.py:65
  198.9 2.7 fusion.3
  201.6 6.0 %fusion.21 = bf16[512,6,128]{0,2,1:T(8,128)(2,1)S(1)} fusion(f32[6,512,1024]{2,1,0:T(8,128)} %get-tuple-element.14, f32[6,512]{1,0:T(8,128)S(1)} %get-tuple-element.13, f32[1024,6,3,128]{0,3,2,1:T(8,128)S(1)} %bitcast.81), kind=kOutput, calls=%fused_computation.37 | convolution fusion | flops 815136768 | bytes 14958592 | tf_op jit(solution)/shard_map/hqk,khe->qhe/dot_general | solution.py:76
  207.6 2.9 fusion.22
  210.7 9.6 %convolution_convert_fusion = bf16[1024,3072]{1,0:T(8,128)(2,1)} fusion(bf16[1024,768]{0,1:T(8,128)(2,1)S(1)} %bitcast.83, bf16[768,3072]{1,0:T(8,128)(2,1)} %all-gather.5.cloned.1.call-done), kind=kOutput, calls=%fused_computation.10 | convolution fusion | flops 4834983936 | bytes 12582912 | tf_op jit(solution)/shard_map/dot_general | solution.py:82
  221.1 111.7 %reduce-scatter.2.cloned.1.call-done = bf16[256,3072]{1,0:T(8,128)(2,1)} async-done(((bf16[1024,3072]{1,0:T(8,128)(2,1)}), bf16[256,3072]{1,0:T(8,128)(2,1)}) %reduce-scatter.2.cloned.1.call-update) | async-done | bytes 1572880 | tf_op jit(solution)/shard_map/reduce_scatter | solution.py:81
  338.9 3.6 collective-permute-start.5
  344.5 2.4 collective-permute-start.7
  349.4 4.3 %collective-permute-start.8 = (bf16[256]{0:T(256)(128)(2,1)S(1)}, bf16[256]{0:T(256)(128)(2,1)S(1)}, u32[]{:S(2)}, u32[]{:S(2)}) collective-permute-start(bf16[256]{0:T(256)(128)(2,1)S(1)} %collective-permute-done.7), channel_id=1, source_target_pairs={{2,0},{3,1},{6,4},{7,5},{10,8},{11,9},{14,12},{15,13},{18,16},{19,... | collective-permute-start | bytes 1544 | tf_op jit(solution)/shard_map/ppermute | solution.py:29
  356.9 5.2 %collective-permute-done.6 = bf16[256,128]{0,1:T(8,128)(2,1)S(1)} collective-permute-done((bf16[256,128]{0,1:T(8,128)(2,1)S(1)}, bf16[256,128]{0,1:T(8,128)(2,1)S(1)}, u32[]{:S(2)}, u32[]{:S(2)}) %collective-permute-start.6) | collective-permute-done | bytes 65568 | tf_op jit(solution)/shard_map/ppermute | solution.py:29
  (77 shorter events, 35.2 us)
Async XLA Ops:
  7.2 328.7 %copy-start = (bf16[3072,64]{0,1:T(8,128)(2,1)S(1)}, bf16[3072,64]{0,1:T(8,128)(2,1)}, u32[]{:S(2)}) copy-start(bf16[3072,64]{0,1:T(8,128)(2,1)} %param.12) | copy-start | bytes 1179652
  7.2 5.6 %copy-start.1 = (bf16[1,256,3072]{2,1,0:T(8,128)(2,1)S(1)}, bf16[1,256,3072]{2,1,0:T(8,128)(2,1)}, u32[]{:S(2)}) copy-start(bf16[1,256,3072]{2,1,0:T(8,128)(2,1)} %param.8) | copy-start | bytes 4718596
  7.2 148.3 %all-gather.3.cloned.1.call-start = ((), (), s32[]{:S(2)}) async-start(), calls=%async_computation.1 | async-start | bytes 7864320 | tf_op jit(solution)/shard_map/all_gather | solution.py:51
  14.8 196.0 %all-gather.5.cloned.1.call-start = ((), (), s32[]{:S(2)}) async-start(), calls=%async_computation.2 | async-start | bytes 5898240 | tf_op jit(solution)/shard_map/all_gather | solution.py:55
  14.8 39.4 %collective-permute-start = (bf16[768,2304]{1,0:T(8,128)(2,1)}, bf16[768,2304]{1,0:T(8,128)(2,1)S(1)}, u32[]{:S(2)}, u32[]{:S(2)}) collective-permute-start(bf16[768,2304]{1,0:T(8,128)(2,1)} %param.10), channel_id=1, source_target_pairs={{0,12},{4,0},{8,4},{12,8},{1,13},{5,1},{9,5},{13,9},{2,14},{6,2},{... | collective-permute-start | bytes 10616840 | tf_op jit(solution)/shard_map/ppermute | solution.py:17
  55.9 41.2 %collective-permute-start.1 = (bf16[768,2304]{1,0:T(8,128)(2,1)S(1)}, bf16[768,2304]{1,0:T(8,128)(2,1)}, u32[]{:S(2)}, u32[]{:S(2)}) collective-permute-start(bf16[768,2304]{1,0:T(8,128)(2,1)S(1)} %collective-permute-done), channel_id=1, source_target_pairs={{0,12},{4,0},{8,4},{12,8},{1,13},{5,1},{9,5},{13,9},{2,14},{6,2},{... | collective-permute-start | bytes 10616840 | tf_op jit(solution)/shard_map/ppermute | solution.py:17
  97.1 41.6 %collective-permute-start.2 = (bf16[768,2304]{1,0:T(8,128)(2,1)}, bf16[768,2304]{1,0:T(8,128)(2,1)}, u32[]{:S(2)}, u32[]{:S(2)}) collective-permute-start(bf16[768,2304]{1,0:T(8,128)(2,1)} %collective-permute-done.1), channel_id=1, source_target_pairs={{0,12},{4,0},{8,4},{12,8},{1,13},{5,1},{9,5},{13,9},{2,14},{6,2},{... | collective-permute-start | bytes 10616840 | tf_op jit(solution)/shard_map/ppermute | solution.py:17
  99.5 233.4 %reduce-scatter.2.cloned.1.call-start = ((), (), s32[]{:S(2)}) async-start(), calls=%async_computation.3 | async-start | bytes 7864320 | tf_op jit(solution)/shard_map/reduce_scatter | solution.py:81
  99.6 4.1 %copy-start.6 = (bf16[768,2304]{1,0:T(8,128)(2,1)S(1)}, bf16[768,2304]{1,0:T(8,128)(2,1)}, u32[]{:S(2)}) copy-start(bf16[768,2304]{1,0:T(8,128)(2,1)} %copy-done.5) | copy-start | bytes 10616836
  109.8 33.6 %copy-start.4 = (bf16[768,2304]{1,0:T(8,128)(2,1)S(1)}, bf16[768,2304]{1,0:T(8,128)(2,1)}, u32[]{:S(2)}) copy-start(bf16[768,2304]{1,0:T(8,128)(2,1)} %param.10) | copy-start | bytes 10616836
  175.2 3.6 copy-start.3
  184.4 5.3 %copy-start.2 = (f32[1024,6,1,128]{3,0,1,2:T(8,128)S(1)}, f32[1024,6,1,128]{3,0,1,2:T(8,128)}, u32[]{:S(2)}) copy-start(f32[1024,6,1,128]{3,0,1,2:T(8,128)} %copy.21) | copy-start | bytes 9437188
  189.7 9.2 %slice-start = ((s8[9437184]{0:T(1024)(128)(4,1)}), s8[4194304]{0:T(1024)(128)(4,1)S(1)}, s32[]{:S(2)}) async-start(s8[9437184]{0:T(1024)(128)(4,1)} %bitcast.78), calls=%async_computation.4 | async-start | bytes 8388608
  190.6 8.2 %slice-start.1 = ((s8[9437184]{0:T(1024)(128)(4,1)}), s8[4194304]{0:T(1024)(128)(4,1)S(1)}, s32[]{:S(2)}) async-start(s8[9437184]{0:T(1024)(128)(4,1)} %bitcast.78), calls=%async_computation.5 | async-start | bytes 8388608
  190.7 8.2 %slice-start.2 = ((s8[9437184]{0:T(1024)(128)(4,1)}), s8[1048576]{0:T(1024)(128)(4,1)S(1)}, s32[]{:S(2)}) async-start(s8[9437184]{0:T(1024)(128)(4,1)} %bitcast.78), calls=%async_computation.6 | async-start | bytes 2097152
  332.9 3.0 copy-start.11
  337.0 16.7 %collective-permute-start.3 = (bf16[256,128]{0,1:T(8,128)(2,1)S(1)}, bf16[256,128]{0,1:T(8,128)(2,1)S(1)}, u32[]{:S(2)}, u32[]{:S(2)}) collective-permute-start(bf16[256,128]{0,1:T(8,128)(2,1)S(1)} %fusion.29), channel_id=1, source_target_pairs={{0,4},{4,8},{8,12},{1,5},{5,9},{9,13},{2,6},{6,10},{10,14},{3,7},{... | collective-permute-start | bytes 196616 | tf_op jit(solution)/shard_map/ppermute | solution.py:29
  338.9 16.1 %collective-permute-start.5 = (bf16[256,128]{0,1:T(8,128)(2,1)S(1)}, bf16[256,128]{0,1:T(8,128)(2,1)S(1)}, u32[]{:S(2)}, u32[]{:S(2)}) collective-permute-start(bf16[256,128]{0,1:T(8,128)(2,1)S(1)} %fusion.29), channel_id=1, source_target_pairs={{4,0},{8,4},{12,8},{5,1},{9,5},{13,9},{6,2},{10,6},{14,10},{7,3},{... | collective-permute-start | bytes 196616 | tf_op jit(solution)/shard_map/ppermute | solution.py:29
  342.6 4.3 %collective-permute-start.9 = (bf16[256]{0:T(256)(128)(2,1)S(1)}, bf16[256]{0:T(256)(128)(2,1)S(1)}, u32[]{:S(2)}, u32[]{:S(2)}) collective-permute-start(bf16[256]{0:T(256)(128)(2,1)S(1)} %convert_element_type.109), channel_id=1, source_target_pairs={{4,0},{8,4},{12,8},{5,1},{9,5},{13,9},{6,2},{10,6},{14,10},{7,3},{... | collective-permute-start | bytes 1544 | tf_op jit(solution)/shard_map/ppermute | solution.py:29
  344.5 4.9 %collective-permute-start.7 = (bf16[256]{0:T(256)(128)(2,1)S(1)}, bf16[256]{0:T(256)(128)(2,1)S(1)}, u32[]{:S(2)}, u32[]{:S(2)}) collective-permute-start(bf16[256]{0:T(256)(128)(2,1)S(1)} %convert_element_type.109), channel_id=1, source_target_pairs={{0,4},{4,8},{8,12},{1,5},{5,9},{9,13},{2,6},{6,10},{10,14},{3,7},{... | collective-permute-start | bytes 1544 | tf_op jit(solution)/shard_map/ppermute | solution.py:29
  346.9 9.4 %collective-permute-start.10 = (bf16[256]{0:T(256)(128)(2,1)S(1)}, bf16[256]{0:T(256)(128)(2,1)S(1)}, u32[]{:S(2)}, u32[]{:S(2)}) collective-permute-start(bf16[256]{0:T(256)(128)(2,1)S(1)} %collective-permute-done.9), channel_id=1, source_target_pairs={{0,2},{1,3},{4,6},{5,7},{8,10},{9,11},{12,14},{13,15},{16,18},{17,... | collective-permute-start | bytes 1544 | tf_op jit(solution)/shard_map/ppermute | solution.py:29
  349.4 6.9 %collective-permute-start.8 = (bf16[256]{0:T(256)(128)(2,1)S(1)}, bf16[256]{0:T(256)(128)(2,1)S(1)}, u32[]{:S(2)}, u32[]{:S(2)}) collective-permute-start(bf16[256]{0:T(256)(128)(2,1)S(1)} %collective-permute-done.7), channel_id=1, source_target_pairs={{2,0},{3,1},{6,4},{7,5},{10,8},{11,9},{14,12},{15,13},{18,16},{19,... | collective-permute-start | bytes 1544 | tf_op jit(solution)/shard_map/ppermute | solution.py:29
  353.7 3.2 collective-permute-start.4
  355.0 7.1 %collective-permute-start.6 = (bf16[256,128]{0,1:T(8,128)(2,1)S(1)}, bf16[256,128]{0,1:T(8,128)(2,1)S(1)}, u32[]{:S(2)}, u32[]{:S(2)}) collective-permute-start(bf16[256,128]{0,1:T(8,128)(2,1)S(1)} %collective-permute-done.5), channel_id=1, source_target_pairs={{0,2},{1,3},{4,6},{5,7},{8,10},{9,11},{12,14},{13,15},{16,18},{17,... | collective-permute-start | bytes 196616 | tf_op jit(solution)/shard_map/ppermute | solution.py:29
  (5 other events, 10.5 us)
Sparse Core Ops, SparseCore 0:
  14.9 113.4 all-gather.2
  129.9 37.5 all-gather.4
  220.5 112.3 reduce-scatter.1
